TPU v7x, 256 devices: a whole 4x4x8 slice. The times are simulated.
256 devices in a mesh: tm: 32 (over y, z), space: 8 (over x, core).
Axes of the slice: x: 4, y: 4, z: 8, core: 2. Of those that a mesh axis runs over, the one named last changes fastest.
Arguments:
- inverse_factor: bfloat16 [2, 32, 4096, 4096], P(None, 'tm', 'space'), may hold values from -1.5 to 1.5, as said below
- tile_mask: int32 [32, 32], replicated, may hold values 0 or 1
- carry_rate: float32 [32, 4096, 2], P('tm', 'space'), may hold values from 0 to 1
- right_side: float32 [32, 4096, 2, 128], P('tm', 'space'), may hold values from -1.5 to 1.5
- arrow_rows: bfloat16 [32, 4096, 2, 512], P('tm', 'space'), may hold values from -0.0625 to 0.0625
- fixed_rhs: float32 [2, 512, 128], P(None, ('tm', 'space')), may hold values from -6 to 6
- tip_factor: bfloat16 [2, 512, 512], replicated, may hold values from -1 to 1, as said below
Outputs:
- solution: float32 [32, 4096, 2, 128], P('tm', 'space')
- fixed_solution: float32 [2, 512, 128], P(None, ('tm', 'space'))
Inputs may be any that keep to these rules, and one draw needn't show every extreme that they name: `tile_mask`: 1 marks a tile that may be nonzero. `inverse_factor`: only entries on or below the diagonal are read. `tip_factor`: only entries on or below the diagonal are read.
All inputs are finite; a program needn't handle non-finite values.
Results may differ from a plain program's by a relative error of at most 0.022.
Values may be sent and summed in bfloat16 or wider, within the bound.
No kernel may reach another device: no remote copies, remote signals or barrier semaphores. Data moves between devices by JAX's collectives and lax.ppermute only.
A program may use at most 320 MiB of HBM per device.

v0:
```python
import jax
import jax.numpy as jnp
from jax import lax
from jax.sharding import PartitionSpec as P

TILE = 128


def carried_in(shard, axis, join, neutral, backward):
    count = lax.axis_size(axis)
    place = lax.axis_index(axis)
    ahead = count - 1 - place if backward else place
    gathered = jax.tree.map(
        lambda a, kind: lax.all_gather(a.astype(kind), axis), shard, (jnp.bfloat16, jnp.bfloat16)
    )
    state = jax.tree.map(lambda a, e: jnp.zeros_like(a) + jnp.asarray(e, a.dtype), shard, neutral)

    def one(turn, state):
        source = count - 1 - turn if backward else turn
        return join(
            state,
            jax.tree.map(
                lambda a, own: lax.dynamic_index_in_dim(a, source, 0, False).astype(own.dtype),
                gathered,
                shard,
            ),
        )

    return lax.fori_loop(0, ahead, one, state)


def combine(earlier, latter):
    rate_new = latter[0] * earlier[0]
    rest = tuple(
        (value_l + latter[0] * value_e for value_l, value_e in zip(latter[1:], earlier[1:]))
    )
    return (rate_new,) + rest


def tile_keep(tile_table, row_start, row_total, col_total):
    tile_count = tile_table.shape[0]
    tile_ids = jnp.arange(tile_count, dtype=jnp.int32)
    row_index = row_start + jnp.arange(row_total, dtype=jnp.int32)
    col_index = jnp.arange(col_total, dtype=jnp.int32)
    row_onehot = (row_index[:, None] // TILE == tile_ids[None, :]).astype(jnp.float32)
    col_onehot = (col_index[:, None] // TILE == tile_ids[None, :]).astype(jnp.float32)
    marked = jnp.dot(jnp.dot(row_onehot, tile_table.astype(jnp.float32)), col_onehot.T)
    return (marked > 0.5) & (row_index[:, None] >= col_index[None, :])


def on_device(inverse_factor, tile_mask, carry_rate, right_side, arrow_rows, fixed_rhs, tip_factor):
    row_count = right_side.shape[1]
    node_total = inverse_factor.shape[3]
    row_start = lax.axis_index("space") * row_count
    tile_table = jnp.maximum(tile_mask, jnp.eye(tile_mask.shape[0], dtype=jnp.int32))
    weights = inverse_factor[:, 0]
    bf_zero = jnp.zeros((), jnp.bfloat16)
    rate_col = carry_rate[0][:, :, None]
    source = right_side[0]
    unit_rate = jnp.ones_like(rate_col)
    earlier_sum = carried_in(
        (rate_col, source), "tm", combine, (unit_rate, jnp.zeros_like(source)), False
    )
    forward = source + rate_col * earlier_sum[1]
    forward_b = forward.astype(jnp.bfloat16)
    row_keep = tile_keep(tile_table, row_start, row_count, node_total)
    masked_rows = jnp.where(row_keep[None], weights, bf_zero)
    block = masked_rows
    inner_rows = jnp.einsum(
        "hrn,nhk->rhk",
        block,
        lax.all_gather(forward_b, "space", axis=0, tiled=True),
        preferred_element_type=jnp.float32,
    ).astype(jnp.bfloat16)
    block = masked_rows
    scaled = lax.psum_scatter(
        jnp.einsum("hrn,rhk->nhk", block, inner_rows, preferred_element_type=jnp.float32).astype(
            jnp.bfloat16
        ),
        "space",
        scatter_dimension=0,
        tiled=True,
    ).astype(jnp.float32)
    arrow_part = arrow_rows[0]
    coupling = jnp.einsum("rhf,rhk->hfk", arrow_part, forward_b, preferred_element_type=jnp.float32)
    share_rows = fixed_rhs.shape[1]
    share_start = lax.axis_index(("tm", "space")) * share_rows
    contrib = -coupling
    own_part = lax.dynamic_slice_in_dim(contrib, share_start, share_rows, 1) + fixed_rhs
    contrib = lax.dynamic_update_slice_in_dim(contrib, own_part, share_start, 1)
    fixed_forward = lax.psum(contrib, ("tm", "space")).astype(jnp.bfloat16)
    fixed_total = tip_factor.shape[1]
    fixed_index = jnp.arange(fixed_total, dtype=jnp.int32)
    lower_tri = fixed_index[:, None] >= fixed_index[None, :]
    tip_lower = jnp.where(lower_tri[None], tip_factor, bf_zero)
    tip_inner = jnp.einsum(
        "hij,hjk->hik", tip_lower, fixed_forward, preferred_element_type=jnp.float32
    ).astype(jnp.bfloat16)
    fixed_solution = jnp.einsum(
        "hij,hik->hjk", tip_lower, tip_inner, preferred_element_type=jnp.float32
    )
    fixed_own = lax.dynamic_slice_in_dim(fixed_solution, share_start, share_rows, 1)
    fixed_b = fixed_solution.astype(jnp.bfloat16)
    carried = scaled - jnp.einsum(
        "rhf,hfk->rhk", arrow_part, fixed_b, preferred_element_type=jnp.float32
    )
    following = carried_in(
        (rate_col, rate_col * carried), "tm", combine, (unit_rate, jnp.zeros_like(carried)), True
    )
    solution = carried + following[1]
    return (solution[None], fixed_own)


def solution(mesh):
    placed = (
        P(None, "tm", "space", None),
        P(),
        P("tm", "space", None),
        P("tm", "space", None, None),
        P("tm", "space", None, None),
        P(None, ("tm", "space"), None),
        P(),
    )
    return jax.shard_map(
        on_device,
        mesh=mesh,
        in_specs=placed,
        out_specs=(P("tm", "space", None, None), P(None, ("tm", "space"), None)),
        check_vma=False,
    )
```

profile of v0, /device:TPU:2, one launch (start us, length us, event | category | flops | bytes accessed | tf_op | source)
XLA Modules:
  0.0 596.0 jit_solution(12626880782622736189)
XLA Ops:
  7.2 1.9 copy.62
  9.2 1.2 copy.34
  11.1 52.1 %all-gather = bf16[32,512,2]{1,2,0:T(2,128)(2,1)S(1)} all-gather(bf16[1,512,2]{1,2,0:T(2,128)(2,1)S(1)} %convert_element_type.103), channel_id=2, replica_groups=mesh['tm'=32,'space'=8] {'tm'}, dimensions={0}, use_global_device_ids=true | all-gather | bytes 67584 | tf_op jit(solution)/shard_map/all_gather | solution.py:14
  63.2 3.3 copy.37
  66.6 46.1 %all-gather.6.cloned.1.call-done = bf16[32,512,2,128]{3,1,2,0:T(8,128)(2,1)} async-done(((bf16[1,512,2,128]{3,1,2,0:T(8,128)(2,1)}), bf16[32,512,2,128]{3,1,2,0:T(8,128)(2,1)}) %all-gather.6.cloned.1.call-update) | async-done | bytes 8388624 | tf_op jit(solution)/shard_map/all_gather | solution.py:14
  114.4 4.2 fusion
  118.6 154.2 %all-gather.8.cloned.1.call-done = bf16[4096,2,128]{0,2,1:T(8,128)(2,1)} async-done(((bf16[512,2,128]{0,2,1:T(8,128)(2,1)}), bf16[4096,2,128]{0,2,1:T(8,128)(2,1)}) %all-gather.8.cloned.1.call-update) | async-done | bytes 2097168 | tf_op jit(solution)/shard_map/all_gather | solution.py:72
  272.7 13.2 %fusion.4 = bf16[4096,2,128]{0,2,1:T(8,128)(2,1)} fusion(bf16[2,1,512,4096]{3,2,1,0:T(8,128)(2,1)} %param.11, pred[512,4096]{1,0:T(8,128)(4,1)} %fusion, bf16[4096,2,128]{0,2,1:T(8,128)(2,1)} %all-gather.8.cloned.1.call-done), kind=kOutput, calls=%fused_computation.12 | convolution fusion | flops 2157051904 | bytes 14680064 | tf_op jit(solution)/shard_map/hrn,rhk->nhk/dot_general | solution.py:77
  286.7 1.1 dynamic_update_slice.3
  287.8 78.9 %all-reduce.1 = bf16[2,512,128]{1,2,0:T(8,128)(2,1)S(1)} all-reduce(f32[2,512,128]{1,2,0:T(8,128)S(1)} %dynamic_update_slice.3), channel_id=1, replica_groups=mesh['tm'=32,'space'=8] {'tm','space'}, use_global_device_ids=true, to_apply=%region_3.4 | all-reduce | flops 131072 | bytes 786432 | tf_op jit(solution)/shard_map/psum | solution.py:91
  366.7 2.3 fusion.9
  369.0 2.1 multiply_convert_fusion
  371.8 102.9 %all-gather.10.cloned.1.call-done = bf16[16384,2,128]{0,2,1:T(8,128)(2,1)} async-done(((bf16[512,2,128]{0,2,1:T(8,128)(2,1)}), bf16[16384,2,128]{0,2,1:T(8,128)(2,1)}) %all-gather.10.cloned.1.call-update) | async-done | bytes 8388624 | tf_op jit(solution)/shard_map/all_gather | solution.py:14
  474.7 21.1 %copy.52 = bf16[16384,2,128]{2,1,0:T(2,128)(2,1)} copy(bf16[16384,2,128]{0,2,1:T(8,128)(2,1)} %all-gather.10.cloned.1.call-done) | data formatting | bytes 16777216 | tf_op jit(solution)/shard_map/while | solution.py:29
  495.9 92.2 %while.27 = (s32[]{:T(128)}, f32[512,2,128]{2,1,0:T(2,128)S(1)}, s32[]{:T(128)}, bf16[32,512,2,128]{3,2,1,0:T(2,128)(2,1)}, bf16[32,512,2,1]{2,1,3,0:T(8,128)(2,...) while((s32[]{:T(128)}, f32[512,2,128]{2,1,0:T(2,128)S(1)}, s32[]{:T(128)}, ...), condition=%wide.region_5.6_spmd, body=%wide.region_4.5_spmd.sunk | while | flops 394246 | bytes 1321107 | solution.py:29
  495.9 0.9 bitcast_convert_fusion.5
  496.9 2.0 convert_add_fusion.5
  498.9 0.9 bitcast_convert_fusion.5
  499.8 2.0 convert_add_fusion.5
  502.8 2.0 convert_add_fusion.5
  505.8 2.0 convert_add_fusion.5
  507.8 0.9 bitcast_convert_fusion.5
  508.8 2.0 convert_add_fusion.5
  510.8 0.9 bitcast_convert_fusion.5
  511.7 2.0 convert_add_fusion.5
  513.8 0.9 bitcast_convert_fusion.5
  514.7 2.0 convert_add_fusion.5
  516.7 0.9 bitcast_convert_fusion.5
  517.7 2.0 convert_add_fusion.5
  520.7 2.0 convert_add_fusion.5
  523.6 2.0 convert_add_fusion.5
  525.7 0.9 bitcast_convert_fusion.5
  526.6 2.0 convert_add_fusion.5
  528.6 0.9 bitcast_convert_fusion.5
  529.6 2.0 convert_add_fusion.5
  531.6 0.9 bitcast_convert_fusion.5
  532.6 2.0 convert_add_fusion.5
  534.6 0.9 bitcast_convert_fusion.5
  535.5 2.0 convert_add_fusion.5
  537.6 0.9 bitcast_convert_fusion.5
  538.5 2.0 convert_add_fusion.5
  541.5 2.0 convert_add_fusion.5
  544.5 2.0 convert_add_fusion.5
  546.5 0.9 bitcast_convert_fusion.5
  547.4 2.0 convert_add_fusion.5
  549.5 0.9 bitcast_convert_fusion.5
  550.4 2.0 convert_add_fusion.5
  552.4 0.9 bitcast_convert_fusion.5
  553.4 2.0 convert_add_fusion.5
  555.4 0.9 bitcast_convert_fusion.5
  556.3 2.0 convert_add_fusion.5
  559.3 2.0 convert_add_fusion.5
  562.3 2.0 convert_add_fusion.5
  564.3 0.9 bitcast_convert_fusion.5
  565.3 2.0 convert_add_fusion.5
  567.3 0.9 bitcast_convert_fusion.5
  568.2 2.0 convert_add_fusion.5
  571.2 2.0 convert_add_fusion.5
  574.2 2.0 convert_add_fusion.5
  577.2 2.0 convert_add_fusion.5
  580.1 2.0 convert_add_fusion.5
  583.1 2.0 convert_add_fusion.5
  586.1 2.0 convert_add_fusion.5
  588.4 1.0 copy.48
  (48 shorter events, 17.2 us)
Async XLA Ops:
  7.2 279.1 %copy-start = (bf16[1,512,2,512]{3,2,1,0:T(2,128)(2,1)S(1)}, bf16[1,512,2,512]{3,2,1,0:T(2,128)(2,1)}, u32[]{:S(2)}) copy-start(bf16[1,512,2,512]{3,2,1,0:T(2,128)(2,1)} %param.15) | copy-start | bytes 3145732
  7.2 105.5 %all-gather.6.cloned.1.call-start = ((), (), s32[]{:S(2)}) async-start(), calls=%async_computation.1 | async-start | bytes 8650752 | tf_op jit(solution)/shard_map/all_gather | solution.py:14
  9.1 263.6 %all-gather.8.cloned.1.call-start = ((), (), s32[]{:S(2)}) async-start(), calls=%async_computation.2 | async-start | bytes 2359296 | tf_op jit(solution)/shard_map/all_gather | solution.py:72
  112.8 0.7 copy-start.2
  112.8 1.6 copy-start.4
  114.3 254.7 %reduce-scatter.2.cloned.1.call-start = ((), (), s32[]{:S(2)}) async-start(), calls=%async_computation.3 | async-start | bytes 2359296 | tf_op jit(solution)/shard_map/reduce_scatter | solution.py:76
  118.6 167.5 %copy-start.3 = (f32[2,2,128]{2,1,0:T(2,128)S(1)}, f32[2,2,128]{2,1,0:T(2,128)}, u32[]{:S(2)}) copy-start(f32[2,2,128]{2,1,0:T(2,128)} %param.16) | copy-start | bytes 6148
  118.6 167.7 %copy-start.1 = (bf16[512,2,128]{0,2,1:T(8,128)(2,1)S(1)}, bf16[512,2,128]{0,2,1:T(8,128)(2,1)}, u32[]{:S(2)}) copy-start(bf16[512,2,128]{0,2,1:T(8,128)(2,1)} %fusion.19) | copy-start | bytes 786436
  286.0 188.7 %all-gather.10.cloned.1.call-start = ((), (), s32[]{:S(2)}) async-start(), calls=%async_computation.4 | async-start | bytes 8650752 | tf_op jit(solution)/shard_map/all_gather | solution.py:14
Sparse Core Ops, SparseCore 0:
  11.2 101.4 all-gather.5
  115.0 157.6 all-gather.7
  286.1 34.6 reduce-scatter.1
  371.3 103.2 all-gather.9
where the time goes:
time: 598 us; the launch traced here: 596 us
  waiting for transfers between devices  303 us (51%)
  blocking collectives  131 us (22%)
  other arithmetic  92.9 us (16%)
  local copies, waits for them, and re-layouts  31.4 us (5%)
  matrix products  22.2 us (4%)
  between operations  14 us (2%)
    all_gather x1, waiting for transfers between devices, on_device(): lax.all_gather(forward_b, 'space', axis=0, tiled=True)  154 us
    all_gather x2, waiting for transfers between devices, carried_in(): lax.all_gather(a.astype(kind), axis)  149 us
    psum x1, blocking collectives, on_device(): fixed_forward = lax.psum(contrib, ('tm', 'space')).astype(jnp.bfloat16)  78.9 us
    add x31, other arithmetic, combine(): value_l + latter[0] * value_e  62.3 us
    all_gather x1, blocking collectives, carried_in(): lax.all_gather(a.astype(kind), axis)  52.1 us
    convert_element_type x31, other arithmetic, one(): lax.dynamic_index_in_dim(a, source, 0, False).astype(own.dtype)  28.8 us
    while x4, local copies, waits for them, and re-layouts, carried_in(): return lax.fori_loop(0, ahead, one, state)  24.8 us
    dot_general x1, matrix products, on_device(): jnp.einsum('hrn,rhk->nhk', block, inner_rows, preferred_element_type=jnp....  13.2 us
  transfers between devices with their start and end apart: 4, of which 3 were waited for; matrix products, arithmetic and copies ran while one was open for 2% of the time, Pallas kernels for 0%

commit v1 on v0

--- a/solution.py
+++ b/solution.py
@@ -4,6 +4,10 @@
 from jax.sharding import PartitionSpec as P
 
 TILE = 128
+
+
+def carry_flows(axis_name, block_here, group_axis):
+    return lax.psum(lax.psum(block_here, axis_name), group_axis)
 
 
 def carried_in(shard, axis, join, neutral, backward):
@@ -88,7 +92,7 @@
     contrib = -coupling
     own_part = lax.dynamic_slice_in_dim(contrib, share_start, share_rows, 1) + fixed_rhs
     contrib = lax.dynamic_update_slice_in_dim(contrib, own_part, share_start, 1)
-    fixed_forward = lax.psum(contrib, ("tm", "space")).astype(jnp.bfloat16)
+    fixed_forward = carry_flows("space", contrib, "tm").astype(jnp.bfloat16)
     fixed_total = tip_factor.shape[1]
     fixed_index = jnp.arange(fixed_total, dtype=jnp.int32)
     lower_tri = fixed_index[:, None] >= fixed_index[None, :]

time: 598 us -> 715 us (1.20)
  blocking collectives: 131 us -> 200 us
  waiting for transfers between devices: 303 us -> 350 us
    psum x1, blocking collectives: 78.9 us -> 148 us  [carry_flows(): return lax.psum(lax.psum(block_here, axis_name), group_axis)]
    psum x0 -> x1, waiting for transfers between devices: none -> 54.2 us  [carry_flows(): return lax.psum(lax.psum(block_here, axis_name), group_axis)]
  transfers between devices with their start and end apart: 4 -> 5, of which waited for: 3 -> 4; matrix products, arithmetic and copies ran while one was open for 2% -> 4% of each run, Pallas kernels for 0% -> 0%
where the time goes in v1:
time: 715 us; the launch traced here: 713 us
  waiting for transfers between devices  350 us (49%)
  blocking collectives  200 us (28%)
  other arithmetic  92.9 us (13%)
  local copies, waits for them, and re-layouts  32.3 us (5%)
  matrix products  22.3 us (3%)
  between operations  14 us (2%)
    all_gather x1, waiting for transfers between devices, on_device(): lax.all_gather(forward_b, 'space', axis=0, tiled=True)  152 us
    psum x1, blocking collectives, carry_flows(): return lax.psum(lax.psum(block_here, axis_name), group_axis)  148 us
    all_gather x2, waiting for transfers between devices, carried_in(): lax.all_gather(a.astype(kind), axis)  144 us
    add x31, other arithmetic, combine(): value_l + latter[0] * value_e  62.3 us
    psum x1, waiting for transfers between devices, carry_flows(): return lax.psum(lax.psum(block_here, axis_name), group_axis)  54.2 us
    all_gather x1, blocking collectives, carried_in(): lax.all_gather(a.astype(kind), axis)  52.1 us
    convert_element_type x31, other arithmetic, one(): lax.dynamic_index_in_dim(a, source, 0, False).astype(own.dtype)  28.8 us
    while x4, local copies, waits for them, and re-layouts, carried_in(): return lax.fori_loop(0, ahead, one, state)  24.9 us
  transfers between devices with their start and end apart: 5, of which 4 were waited for; matrix products, arithmetic and copies ran while one was open for 4% of the time, Pallas kernels for 0%

profile of v1, /device:TPU:2, one launch (start us, length us, event | category | flops | bytes accessed | tf_op | source)
XLA Modules:
  0.0 712.8 jit_solution(9388366884239099188)
XLA Ops:
  7.2 1.9 copy.62
  9.2 1.2 copy.34
  11.1 52.1 %all-gather = bf16[32,512,2]{1,2,0:T(2,128)(2,1)S(1)} all-gather(bf16[1,512,2]{1,2,0:T(2,128)(2,1)S(1)} %convert_element_type.103), channel_id=2, replica_groups=mesh['tm'=32,'space'=8] {'tm'}, dimensions={0}, use_global_device_ids=true | all-gather | bytes 67584 | tf_op jit(solution)/shard_map/all_gather | solution.py:18
  63.2 3.3 copy.37
  66.6 46.1 %all-gather.6.cloned.1.call-done = bf16[32,512,2,128]{3,1,2,0:T(8,128)(2,1)} async-done(((bf16[1,512,2,128]{3,1,2,0:T(8,128)(2,1)}), bf16[32,512,2,128]{3,1,2,0:T(8,128)(2,1)}) %all-gather.6.cloned.1.call-update) | async-done | bytes 8388624 | tf_op jit(solution)/shard_map/all_gather | solution.py:18
  114.6 4.2 fusion
  119.2 1.1 dynamic_update_slice.3
  121.1 151.6 %all-gather.8.cloned.1.call-done = bf16[4096,2,128]{0,2,1:T(8,128)(2,1)} async-done(((bf16[512,2,128]{0,2,1:T(8,128)(2,1)}), bf16[4096,2,128]{0,2,1:T(8,128)(2,1)}) %all-gather.8.cloned.1.call-update) | async-done | bytes 2097168 | tf_op jit(solution)/shard_map/all_gather | solution.py:76
  272.7 13.4 %fusion.4 = bf16[4096,2,128]{0,2,1:T(8,128)(2,1)} fusion(bf16[2,1,512,4096]{3,2,1,0:T(8,128)(2,1)} %param.11, pred[512,4096]{1,0:T(8,128)(4,1)} %fusion, bf16[4096,2,128]{0,2,1:T(8,128)(2,1)} %all-gather.8.cloned.1.call-done), kind=kOutput, calls=%fused_computation.12 | convolution fusion | flops 2157051904 | bytes 14680064 | tf_op jit(solution)/shard_map/hrn,rhk->nhk/dot_general | solution.py:81
  286.3 54.2 %all-reduce.3.cloned.1.call-done = f32[2,512,128]{1,2,0:T(8,128)} async-done(((f32[2,512,128]{1,2,0:T(8,128)}), f32[2,512,128]{1,2,0:T(8,128)}) %all-reduce.3.cloned.1.call-update) | async-done | bytes 524304 | tf_op jit(solution)/shard_map/psum | solution.py:10
  340.5 148.3 %all-reduce.4 = bf16[2,512,128]{1,2,0:T(8,128)(2,1)S(1)} all-reduce(f32[2,512,128]{1,2,0:T(8,128)} %all-reduce.3.cloned.1.call-done), channel_id=1, replica_groups=mesh['tm'=32,'space'=8] {'tm'}, use_global_device_ids=true, to_apply=%region_4.5 | all-reduce | flops 131072 | bytes 786432 | tf_op jit(solution)/shard_map/psum | solution.py:10
  488.8 2.3 fusion.9
  491.2 2.1 multiply_convert_fusion
  494.0 97.6 %all-gather.10.cloned.1.call-done = bf16[16384,2,128]{0,2,1:T(8,128)(2,1)} async-done(((bf16[512,2,128]{0,2,1:T(8,128)(2,1)}), bf16[16384,2,128]{0,2,1:T(8,128)(2,1)}) %all-gather.10.cloned.1.call-update) | async-done | bytes 8388624 | tf_op jit(solution)/shard_map/all_gather | solution.py:18
  591.5 21.1 %copy.52 = bf16[16384,2,128]{2,1,0:T(2,128)(2,1)} copy(bf16[16384,2,128]{0,2,1:T(8,128)(2,1)} %all-gather.10.cloned.1.call-done) | data formatting | bytes 16777216 | tf_op jit(solution)/shard_map/while | solution.py:33
  612.8 92.2 %while.27 = (s32[]{:T(128)}, f32[512,2,128]{2,1,0:T(2,128)S(1)}, s32[]{:T(128)}, bf16[32,512,2,128]{3,2,1,0:T(2,128)(2,1)}, bf16[32,512,2,1]{2,1,3,0:T(8,128)(2,...) while((s32[]{:T(128)}, f32[512,2,128]{2,1,0:T(2,128)S(1)}, s32[]{:T(128)}, ...), condition=%wide.region_6.7_spmd, body=%wide.region_5.6_spmd.sunk | while | flops 394246 | bytes 1321107 | solution.py:33
  612.8 0.9 bitcast_convert_fusion.5
  613.7 2.0 convert_add_fusion.5
  616.7 2.0 convert_add_fusion.5
  619.7 2.0 convert_add_fusion.5
  621.7 0.9 bitcast_convert_fusion.5
  622.6 2.0 convert_add_fusion.5
  624.7 0.9 bitcast_convert_fusion.5
  625.6 2.0 convert_add_fusion.5
  627.7 0.9 bitcast_convert_fusion.5
  628.6 2.0 convert_add_fusion.5
  630.6 0.9 bitcast_convert_fusion.5
  631.6 2.0 convert_add_fusion.5
  634.5 2.0 convert_add_fusion.5
  637.5 2.0 convert_add_fusion.5
  639.6 0.9 bitcast_convert_fusion.5
  640.5 2.0 convert_add_fusion.5
  642.5 0.9 bitcast_convert_fusion.5
  643.5 2.0 convert_add_fusion.5
  645.5 0.9 bitcast_convert_fusion.5
  646.4 2.0 convert_add_fusion.5
  648.5 0.9 bitcast_convert_fusion.5
  649.4 2.0 convert_add_fusion.5
  652.4 2.0 convert_add_fusion.5
  655.4 2.0 convert_add_fusion.5
  657.4 0.9 bitcast_convert_fusion.5
  658.3 2.0 convert_add_fusion.5
  660.4 0.9 bitcast_convert_fusion.5
  661.3 2.0 convert_add_fusion.5
  663.4 0.9 bitcast_convert_fusion.5
  664.3 2.0 convert_add_fusion.5
  666.3 0.9 bitcast_convert_fusion.5
  667.3 2.0 convert_add_fusion.5
  669.3 0.9 bitcast_convert_fusion.5
  670.2 2.0 convert_add_fusion.5
  673.2 2.0 convert_add_fusion.5
  676.2 2.0 convert_add_fusion.5
  678.2 0.9 bitcast_convert_fusion.5
  679.2 2.0 convert_add_fusion.5
  681.2 0.9 bitcast_convert_fusion.5
  682.1 2.0 convert_add_fusion.5
  685.1 2.0 convert_add_fusion.5
  688.1 2.0 convert_add_fusion.5
  691.1 2.0 convert_add_fusion.5
  694.0 2.0 convert_add_fusion.5
  697.0 2.0 convert_add_fusion.5
  700.0 2.0 convert_add_fusion.5
  703.0 2.0 convert_add_fusion.5
  705.3 1.0 copy.48
  (53 shorter events, 19.0 us)
Async XLA Ops:
  7.2 111.6 %copy-start = (bf16[1,512,2,512]{3,2,1,0:T(2,128)(2,1)S(1)}, bf16[1,512,2,512]{3,2,1,0:T(2,128)(2,1)}, u32[]{:S(2)}) copy-start(bf16[1,512,2,512]{3,2,1,0:T(2,128)(2,1)} %param.15) | copy-start | bytes 3145732
  7.2 105.5 %all-gather.6.cloned.1.call-start = ((), (), s32[]{:S(2)}) async-start(), calls=%async_computation.1 | async-start | bytes 8650752 | tf_op jit(solution)/shard_map/all_gather | solution.py:18
  9.1 263.6 %all-gather.8.cloned.1.call-start = ((), (), s32[]{:S(2)}) async-start(), calls=%async_computation.2 | async-start | bytes 2359296 | tf_op jit(solution)/shard_map/all_gather | solution.py:76
  112.8 0.7 copy-start.3
  112.8 1.6 copy-start.4
  112.8 1.7 copy-start.5
  114.3 226.2 %all-reduce.3.cloned.1.call-start = ((), (), s32[]{:S(2)}) async-start(), calls=%async_computation.4 | async-start | bytes 1048576 | tf_op jit(solution)/shard_map/psum | solution.py:10
  114.5 4.2 copy-start.2
  120.2 0.8 copy-start.1
  121.1 370.1 %reduce-scatter.2.cloned.1.call-start = ((), (), s32[]{:S(2)}) async-start(), calls=%async_computation.3 | async-start | bytes 2359296 | tf_op jit(solution)/shard_map/reduce_scatter | solution.py:80
  286.1 305.4 %all-gather.10.cloned.1.call-start = ((), (), s32[]{:S(2)}) async-start(), calls=%async_computation.5 | async-start | bytes 8650752 | tf_op jit(solution)/shard_map/all_gather | solution.py:18
Sparse Core Ops, SparseCore 0:
  11.2 101.4 all-gather.5
  114.5 158.2 all-gather.7
  275.7 64.8 all-reduce.2
  343.1 34.5 reduce-scatter.1
  493.5 97.9 all-gather.9
